TPU v7x, 32 devices: a whole 2x2x4 slice. The times are simulated.
32 devices in a mesh: section: 2 (over x), dp: 4 (over y, core), expert: 4 (over z).
Axes of the slice: x: 2, y: 2, z: 4, core: 2. Of those that a mesh axis runs over, the one named last changes fastest.
Arguments:
- tokens: bfloat16 [2, 2048, 2560], P('section', ('dp', 'expert')), may hold values from -6 to 6
- cotangent: bfloat16 [2, 2048, 2560], P('section', ('dp', 'expert')), may hold values from -3 to 3
- routes: int32 [2, 2048, 6], P('section', ('dp', 'expert')), may hold values from 0 to 159, as said below
- gates: float32 [2, 2048, 6], P('section', ('dp', 'expert')), may hold values from 0.2 to 1
- gate_up: bfloat16 [2, 4, 2, 1024, 2560], P('section', 'expert', None, 'dp'), may hold values from -0.125 to 0.125
- down: bfloat16 [2, 4, 1024, 2560], P('section', 'expert', 'dp'), may hold values from -0.1875 to 0.1875
Outputs:
- handed_on: bfloat16 [2, 2048, 2560], P('section', ('dp', 'expert'))
- handed_back: bfloat16 [2, 2048, 2560], P('section', ('dp', 'expert'))
- grad_gate_up: bfloat16 [2, 4, 2, 1024, 2560], P('section', 'expert', None, 'dp')
- grad_down: bfloat16 [2, 4, 1024, 2560], P('section', 'expert', 'dp')
Inputs may be any that keep to these rules, and one draw needn't show every extreme that they name: `routes`: A token's 6 ids are distinct and at most one of them is below 4. In each device's block of 128 tokens no id below 4 is named by more than 32 tokens.
All inputs are finite; a program needn't handle non-finite values.
Results may differ from a plain program's by a relative error of at most 0.0065.
Values may be sent and summed in bfloat16 or wider, within the bound.
No kernel may reach another device: no remote copies, remote signals or barrier semaphores. Data moves between devices by JAX's collectives and lax.ppermute only.
A program may use at most 64 MiB of HBM per device.

v0:
```python
import jax
import jax.numpy as jnp
from jax import lax
from jax.sharding import PartitionSpec as P


def passed_along(value, axis, steps):
    count = lax.axis_size(axis)
    first, last = (max(0, -steps), min(count, count - steps))
    return lax.ppermute(value, axis, [(source, source + steps) for source in range(first, last)])


def to_experts(buffer):
    columns = lax.all_to_all(buffer, "expert", split_axis=0, concat_axis=0, tiled=True)
    arrived = lax.all_gather(columns, "dp", axis=0, tiled=True)
    return arrived


def to_owners(partial_value):
    copies = lax.axis_size("dp")
    quarters = lax.all_to_all(partial_value, "dp", split_axis=0, concat_axis=0, tiled=True)
    quarters = quarters.reshape((copies, quarters.shape[0] // copies) + quarters.shape[1:])
    column_rows = jnp.sum(quarters.astype(jnp.float32), 0).astype(jnp.bfloat16)
    summed = lax.all_to_all(column_rows, "expert", split_axis=0, concat_axis=0, tiled=True)
    return summed


def shards(tokens, cotangent, routes, gates, gate_up, down):
    window = lax.axis_size("expert")
    copies = lax.axis_size("dp")
    rows_here = tokens.shape[1]
    model_width = tokens.shape[2]
    capacity = rows_here // window
    in_window = routes[0] < window
    expert_of = jnp.sum(jnp.where(in_window, routes[0], 0), -1)
    present = jnp.any(in_window, -1)
    weight = jnp.sum(jnp.where(in_window, gates[0], 0.0), -1)
    member = ((expert_of[:, None] == jnp.arange(window)[None, :]) & present[:, None]).astype(
        jnp.float32
    )
    before = jnp.cumsum(member, 0) - member
    slot_index = jnp.sum(before * member, -1)
    slot_values = jnp.arange(capacity, dtype=jnp.float32)
    select = member.T[:, None, :] * (slot_index[None, None, :] == slot_values[None, :, None])
    select = select.astype(jnp.bfloat16).reshape(window * capacity, rows_here)
    contract_last = (((1,), (1,)), ((), ()))
    contract_first = (((0,), (0,)), ((), ()))

    def to_slots(values):
        packed = jnp.dot(select, values, preferred_element_type=jnp.float32).astype(jnp.bfloat16)
        arrived = to_experts(packed.reshape(window, capacity, model_width))
        return arrived.reshape(copies * window * capacity, model_width)

    def from_slots(partial_value):
        rounded = partial_value.astype(jnp.bfloat16).reshape(copies * window, capacity, model_width)
        owner_rows = to_owners(rounded).reshape(window * capacity, model_width)
        return lax.dot_general(
            select, owner_rows, contract_first, preferred_element_type=jnp.float32
        )

    gate_matrix = gate_up[0, 0, 0]
    up_matrix = gate_up[0, 0, 1]
    down_matrix = down[0, 0]
    slot_rows = to_slots(tokens[0])
    pre_gate = lax.dot_general(
        slot_rows, gate_matrix, contract_last, preferred_element_type=jnp.float32
    )
    pre_up = lax.dot_general(
        slot_rows, up_matrix, contract_last, preferred_element_type=jnp.float32
    )
    sigmoid_gate = jax.nn.sigmoid(pre_gate)
    activated = pre_gate * sigmoid_gate
    hidden = (activated * pre_up).astype(jnp.bfloat16)
    partial_value = jnp.dot(hidden, down_matrix, preferred_element_type=jnp.float32)
    mixture = (from_slots(partial_value) * weight[:, None]).astype(jnp.bfloat16)
    handed_on = passed_along(mixture[None], "section", 1)
    scaled = (cotangent[0].astype(jnp.float32) * weight[:, None]).astype(jnp.bfloat16)
    slot_grads = to_slots(scaled)
    hidden_grad = lax.dot_general(
        slot_grads, down_matrix, contract_last, preferred_element_type=jnp.float32
    )
    grad_down = lax.dot_general(
        hidden, slot_grads, contract_first, preferred_element_type=jnp.float32
    ).astype(jnp.bfloat16)
    gate_slope = sigmoid_gate * (1.0 + pre_gate * (1.0 - sigmoid_gate))
    gate_grad = (hidden_grad * pre_up * gate_slope).astype(jnp.bfloat16)
    up_grad = (hidden_grad * activated).astype(jnp.bfloat16)
    grad_gate = lax.dot_general(
        gate_grad, slot_rows, contract_first, preferred_element_type=jnp.float32
    ).astype(jnp.bfloat16)
    grad_up = lax.dot_general(
        up_grad, slot_rows, contract_first, preferred_element_type=jnp.float32
    ).astype(jnp.bfloat16)
    input_part = jnp.dot(gate_grad, gate_matrix, preferred_element_type=jnp.float32)
    input_part = input_part + jnp.dot(up_grad, up_matrix, preferred_element_type=jnp.float32)
    input_grad = from_slots(input_part).astype(jnp.bfloat16)
    handed_back = passed_along(input_grad[None], "section", -1)
    grads_pair = jnp.stack([grad_gate, grad_up])[None, None]
    return (handed_on, handed_back, grads_pair, grad_down[None, None])


def solution(mesh):
    in_specs = (
        P("section", ("dp", "expert"), None),
        P("section", ("dp", "expert"), None),
        P("section", ("dp", "expert"), None),
        P("section", ("dp", "expert"), None),
        P("section", "expert", None, "dp", None),
        P("section", "expert", "dp", None),
    )
    out_specs = (
        P("section", ("dp", "expert"), None),
        P("section", ("dp", "expert"), None),
        P("section", "expert", None, "dp", None),
        P("section", "expert", "dp", None),
    )
    return jax.shard_map(shards, mesh=mesh, in_specs=in_specs, out_specs=out_specs, check_vma=False)
```

profile of v0, /device:TPU:0, one launch (start us, length us, event | category | flops | bytes accessed | tf_op | source)
XLA Modules:
  0.0 233.5 jit_solution(1484516350349944796)
XLA Ops:
  10.7 23.5 %all_to_all.30 = bf16[4,32,2560]{2,1,0:T(8,128)(2,1)} all-to-all(bf16[4,32,2560]{2,1,0:T(8,128)(2,1)S(1)} %bitcast.96), channel_id=1, replica_groups=mesh['section'=2,'dp'=4,'expert'=4] {'expert'}, dimensions={0} | all-to-all | bytes 1310720 | tf_op jit(solution)/shard_map/all_to_all | solution.py:14
  34.8 19.6 %all_to_all.31 = bf16[4,32,2560]{2,1,0:T(8,128)(2,1)} all-to-all(bf16[4,32,2560]{2,1,0:T(8,128)(2,1)S(1)} %bitcast.95), channel_id=1, replica_groups=mesh['section'=2,'dp'=4,'expert'=4] {'expert'}, dimensions={0} | all-to-all | bytes 1310720 | tf_op jit(solution)/shard_map/all_to_all | solution.py:14
  54.4 4.6 %all-gather.3.cloned.1.call-done = bf16[16,32,2560]{2,1,0:T(8,128)(2,1)} async-done(((bf16[4,32,2560]{2,1,0:T(8,128)(2,1)}), bf16[16,32,2560]{2,1,0:T(8,128)(2,1)}) %all-gather.3.cloned.1.call-update) | async-done | bytes 2621456 | tf_op jit(solution)/shard_map/all_gather | solution.py:15
  59.1 3.1 %fusion.12 = f32[512,256]{1,0:T(8,128)S(1)} fusion(bf16[512,2560]{1,0:T(8,128)(2,1)} %bitcast.91, bf16[1,1,2,256,2560]{4,3,2,1,0:T(8,128)(2,1)} %param.10), kind=kOutput, calls=%fused_computation.22 | convolution fusion | flops 671088640 | bytes 4456448 | tf_op jit(solution)/shard_map/dot_general | solution.py:68
  63.7 22.5 %all-gather.5.cloned.1.call-done = bf16[16,32,2560]{2,1,0:T(8,128)(2,1)} async-done(((bf16[4,32,2560]{2,1,0:T(8,128)(2,1)}), bf16[16,32,2560]{2,1,0:T(8,128)(2,1)}) %all-gather.5.cloned.1.call-update) | async-done | bytes 2621456 | tf_op jit(solution)/shard_map/all_gather | solution.py:15
  86.2 2.7 %multiply_convert_fusion.1 = (bf16[512,256]{1,0:T(8,128)(2,1)S(1)}, bf16[512,256]{1,0:T(8,128)(2,1)S(1)}, bf16[512,256]{1,0:T(8,128)(2,1)S(1)}) fusion(f32[512,256]{1,0:T(8,128)S(1)} %fusion.16, f32[512,256]{1,0:T(8,128)S(1)} %fusion.12, bf16[512,2560]{1,0:T(8,128)(2,1)} %bitcast.97, bf16[1,1,256,2560]{3,2,1,0:T(8,128)(2,1)S(1)} %copy-done), kind=kOutput, calls=%fused_computation.36 | convolution fusion | flops 673054720 | bytes 5767168 | tf_op jit(solution)/shard_map/dot_general | solution.py:79
  88.9 2.3 %convolution_convert_fusion = bf16[512,2560]{1,0:T(8,128)(2,1)} fusion(bf16[512,256]{1,0:T(8,128)(2,1)S(1)} %get-tuple-element.6, bf16[1,1,256,2560]{3,2,1,0:T(8,128)(2,1)S(1)} %copy-done), kind=kOutput, calls=%fused_computation.1 | convolution fusion | flops 672399360 | bytes 4194304 | tf_op jit(solution)/shard_map/dot_general | solution.py:74
  91.3 4.6 %all-to-all-start.1 = ((bf16[16,32,2560]{2,1,0:T(8,128)(2,1)}), bf16[16,32,2560]{2,1,0:T(8,128)(2,1)}, u32[]{:S(2)}, u32[]{:S(2)}) async-start(bf16[16,32,2560]{2,1,0:T(8,128)(2,1)} %bitcast.89), calls=%async_computation.1 | async-start | bytes 5242880 | tf_op jit(solution)/shard_map/all_to_all | solution.py:21
  95.9 2.3 fusion.14
  98.2 2.4 %add_convert_fusion = bf16[512,2560]{1,0:T(8,128)(2,1)} fusion(f32[512,2560]{1,0:T(8,128)S(1)} %fusion.14, bf16[512,256]{1,0:T(8,128)(2,1)S(1)} %get-tuple-element.4, bf16[1,1,2,256,2560]{4,3,2,1,0:T(8,128)(2,1)S(1)} %copy-done.4), kind=kOutput, calls=%fused_computation | convolution fusion | flops 673710080 | bytes 9437184 | tf_op jit(solution)/shard_map/dot_general | solution.py:95
  100.6 26.6 %all-to-all-done.1 = bf16[16,32,2560]{2,1,0:T(8,128)(2,1)} async-done(((bf16[16,32,2560]{2,1,0:T(8,128)(2,1)}), bf16[16,32,2560]{2,1,0:T(8,128)(2,1)}, u32[]{:S(2)}, u32[]{:S(2)}) %all-to-all-start.1) | async-done | bytes 2621472 | tf_op jit(solution)/shard_map/all_to_all | solution.py:21
  127.2 4.6 %all-to-all-start.4 = ((bf16[16,32,2560]{2,1,0:T(8,128)(2,1)}), bf16[16,32,2560]{2,1,0:T(8,128)(2,1)}, u32[]{:S(2)}, u32[]{:S(2)}) async-start(bf16[16,32,2560]{2,1,0:T(8,128)(2,1)} %bitcast.90), calls=%async_computation.4 | async-start | bytes 5242880 | tf_op jit(solution)/shard_map/all_to_all | solution.py:21
  131.8 3.1 %reduce_sum.53 = bf16[4,32,2560]{2,1,0:T(8,128)(2,1)} reduce(bf16[4,4,32,2560]{3,2,1,0:T(8,128)(2,1)} %bitcast.8, bf16[]{:T(256)} %constant.16.clone.1), dimensions={0}, to_apply=%region_4.5 | reduce | flops 983040 | bytes 3276802 | tf_op jit(solution)/shard_map/reduce_sum | solution.py:23
  135.0 28.2 %all-to-all-done.4 = bf16[16,32,2560]{2,1,0:T(8,128)(2,1)} async-done(((bf16[16,32,2560]{2,1,0:T(8,128)(2,1)}), bf16[16,32,2560]{2,1,0:T(8,128)(2,1)}, u32[]{:S(2)}, u32[]{:S(2)}) %all-to-all-start.4) | async-done | bytes 2621472 | tf_op jit(solution)/shard_map/all_to_all | solution.py:21
  163.2 4.6 %all-to-all-start.2 = ((bf16[4,32,2560]{2,1,0:T(8,128)(2,1)}), bf16[4,32,2560]{2,1,0:T(8,128)(2,1)S(1)}, u32[]{:S(2)}, u32[]{:S(2)}) async-start(bf16[4,32,2560]{2,1,0:T(8,128)(2,1)} %reduce_sum.53), calls=%async_computation.2 | async-start | bytes 1310720 | tf_op jit(solution)/shard_map/all_to_all | solution.py:24
  167.8 3.1 %reduce_sum.55 = bf16[4,32,2560]{2,1,0:T(8,128)(2,1)} reduce(bf16[4,4,32,2560]{3,2,1,0:T(8,128)(2,1)} %bitcast.15, bf16[]{:T(256)} %constant.16.clone.1), dimensions={0}, to_apply=%region_6.7 | reduce | flops 983040 | bytes 3276802 | tf_op jit(solution)/shard_map/reduce_sum | solution.py:23
  170.9 13.9 %all-to-all-done.2 = bf16[4,32,2560]{2,1,0:T(8,128)(2,1)S(1)} async-done(((bf16[4,32,2560]{2,1,0:T(8,128)(2,1)}), bf16[4,32,2560]{2,1,0:T(8,128)(2,1)S(1)}, u32[]{:S(2)}, u32[]{:S(2)}) %all-to-all-start.2) | async-done | bytes 655392 | tf_op jit(solution)/shard_map/all_to_all | solution.py:24
  184.8 4.2 %all-to-all-start.5 = ((bf16[4,32,2560]{2,1,0:T(8,128)(2,1)}), bf16[4,32,2560]{2,1,0:T(8,128)(2,1)}, u32[]{:S(2)}, u32[]{:S(2)}) async-start(bf16[4,32,2560]{2,1,0:T(8,128)(2,1)} %reduce_sum.55), calls=%async_computation.5 | async-start | bytes 1310720 | tf_op jit(solution)/shard_map/all_to_all | solution.py:24
  189.0 3.8 %fusion.2 = bf16[1,1,256,2560]{3,2,1,0:T(8,128)(2,1)} fusion(bf16[512,256]{1,0:T(8,128)(2,1)S(1)} %get-tuple-element.6, bf16[512,2560]{1,0:T(8,128)(2,1)} %bitcast.98), kind=kOutput, calls=%fused_computation.7 | convolution fusion | flops 671744000 | bytes 4194304 | tf_op jit(solution)/shard_map/dot_general | solution.py:82
  192.8 1.8 fusion.1
  195.8 3.4 %collective-permute-start = (bf16[1,128,2560]{2,1,0:T(8,128)(2,1)}, bf16[1,128,2560]{2,1,0:T(8,128)(2,1)S(1)}, u32[]{:S(2)}, u32[]{:S(2)}) collective-permute-start(bf16[1,128,2560]{2,1,0:T(8,128)(2,1)} %fusion.6), channel_id=1, source_target_pairs={{0,16},{1,17},{2,18},{3,19},{4,20},{5,21},{6,22},{7,23},{8,24},{9,... | collective-permute-start | bytes 1966088 | tf_op jit(solution)/shard_map/ppermute | solution.py:10
  199.3 6.6 %all-to-all-done.5 = bf16[4,32,2560]{2,1,0:T(8,128)(2,1)} async-done(((bf16[4,32,2560]{2,1,0:T(8,128)(2,1)}), bf16[4,32,2560]{2,1,0:T(8,128)(2,1)}, u32[]{:S(2)}, u32[]{:S(2)}) %all-to-all-start.5) | async-done | bytes 655392 | tf_op jit(solution)/shard_map/all_to_all | solution.py:24
  208.6 2.6 %fusion = bf16[1,256,2560]{2,1,0:T(8,128)(2,1)S(1)} fusion(bf16[512,256]{1,0:T(8,128)(2,1)S(1)} %get-tuple-element.5, bf16[512,2560]{1,0:T(8,128)(2,1)} %bitcast.92), kind=kOutput, calls=%fused_computation.5 | convolution fusion | flops 671744000 | bytes 4194304 | tf_op jit(solution)/shard_map/dot_general | solution.py:88
  213.0 12.0 %collective-permute-done.1 = bf16[1,128,2560]{2,1,0:T(8,128)(2,1)S(1)} collective-permute-done((bf16[1,128,2560]{2,1,0:T(8,128)(2,1)S(1)}, bf16[1,128,2560]{2,1,0:T(8,128)(2,1)S(1)}, u32[]{:S(2)}, u32[]{:S(2)}) %collective-permute-start.1) | collective-permute-done | bytes 655392 | tf_op jit(solution)/shard_map/ppermute | solution.py:10
  (49 shorter events, 12.8 us)
Async XLA Ops:
  7.2 79.1 %copy-start = (bf16[1,1,256,2560]{3,2,1,0:T(8,128)(2,1)S(1)}, bf16[1,1,256,2560]{3,2,1,0:T(8,128)(2,1)}, u32[]{:S(2)}) copy-start(bf16[1,1,256,2560]{3,2,1,0:T(8,128)(2,1)} %param.11) | copy-start | bytes 3932164
  7.2 27.2 %copy-start.9 = (s32[1,128,6]{1,0,2:T(1,128)S(1)}, s32[1,128,6]{1,0,2:T(1,128)}, u32[]{:S(2)}) copy-start(s32[1,128,6]{1,0,2:T(1,128)} %param.8) | copy-start | bytes 9220
  7.2 27.2 %copy-start.12 = (f32[1,128,6]{1,0,2:T(1,128)S(1)}, f32[1,128,6]{1,0,2:T(1,128)}, u32[]{:S(2)}) copy-start(f32[1,128,6]{1,0,2:T(1,128)} %param.9) | copy-start | bytes 9220
  7.2 27.2 %copy-start.6 = (bf16[1,128,2560]{2,1,0:T(8,128)(2,1)S(1)}, bf16[1,128,2560]{2,1,0:T(8,128)(2,1)}, u32[]{:S(2)}) copy-start(bf16[1,128,2560]{2,1,0:T(8,128)(2,1)} %param.7) | copy-start | bytes 1966084
  7.2 51.9 %all-gather.3.cloned.1.call-start = ((), (), s32[]{:S(2)}) async-start(), calls=%async_computation.6 | async-start | bytes 3276800 | tf_op jit(solution)/shard_map/all_gather | solution.py:15
  8.8 45.6 %copy-start.7 = (f32[4,128]{1,0:T(4,128)}, f32[4,128]{1,0:T(4,128)S(1)}, u32[]{:S(2)}) copy-start(f32[4,128]{1,0:T(4,128)S(1)} %fusion.33) | copy-start | bytes 6148
  34.3 51.9 %all-gather.5.cloned.1.call-start = ((), (), s32[]{:S(2)}) async-start(), calls=%async_computation.7 | async-start | bytes 3276800 | tf_op jit(solution)/shard_map/all_gather | solution.py:15
  34.4 27.8 %copy-start.10 = (f32[128]{0:T(128)}, f32[128]{0:T(128)S(1)}, u32[]{:S(2)}) copy-start(f32[128]{0:T(128)S(1)} %fusion.30) | copy-start | bytes 1540
  59.1 3.1 %copy-start.1 = (bf16[16,32,2560]{2,1,0:T(8,128)(2,1)S(1)}, bf16[16,32,2560]{2,1,0:T(8,128)(2,1)}, u32[]{:S(2)}) copy-start(bf16[16,32,2560]{2,1,0:T(8,128)(2,1)} %all-gather.3.cloned.1.call-done) | copy-start | bytes 7864324
  59.1 3.7 %copy-start.3 = (bf16[1,1,2,256,2560]{4,3,2,1,0:T(8,128)(2,1)S(1)}, bf16[1,1,2,256,2560]{4,3,2,1,0:T(8,128)(2,1)}, u32[]{:S(2)}) copy-start(bf16[1,1,2,256,2560]{4,3,2,1,0:T(8,128)(2,1)} %param.10) | copy-start | bytes 7864324
  88.9 9.3 %copy-start.5 = (bf16[512,256]{1,0:T(8,128)(2,1)}, bf16[512,256]{1,0:T(8,128)(2,1)S(1)}, u32[]{:S(2)}) copy-start(bf16[512,256]{1,0:T(8,128)(2,1)S(1)} %get-tuple-element.4) | copy-start | bytes 786436
  91.3 35.9 %all-to-all-start.1 = ((bf16[16,32,2560]{2,1,0:T(8,128)(2,1)}), bf16[16,32,2560]{2,1,0:T(8,128)(2,1)}, u32[]{:S(2)}, u32[]{:S(2)}) async-start(bf16[16,32,2560]{2,1,0:T(8,128)(2,1)} %bitcast.89), calls=%async_computation.1 | async-start | bytes 5242880 | tf_op jit(solution)/shard_map/all_to_all | solution.py:21
  95.9 2.3 %copy-start.4 = (bf16[1,1,2,256,2560]{4,3,2,1,0:T(8,128)(2,1)S(1)}, bf16[1,1,2,256,2560]{4,3,2,1,0:T(8,128)(2,1)}, u32[]{:S(2)}) copy-start(bf16[1,1,2,256,2560]{4,3,2,1,0:T(8,128)(2,1)} %param.10) | copy-start | bytes 7864324
  127.2 36.0 %all-to-all-start.4 = ((bf16[16,32,2560]{2,1,0:T(8,128)(2,1)}), bf16[16,32,2560]{2,1,0:T(8,128)(2,1)}, u32[]{:S(2)}, u32[]{:S(2)}) async-start(bf16[16,32,2560]{2,1,0:T(8,128)(2,1)} %bitcast.90), calls=%async_computation.4 | async-start | bytes 5242880 | tf_op jit(solution)/shard_map/all_to_all | solution.py:21
  163.2 21.6 %all-to-all-start.2 = ((bf16[4,32,2560]{2,1,0:T(8,128)(2,1)}), bf16[4,32,2560]{2,1,0:T(8,128)(2,1)S(1)}, u32[]{:S(2)}, u32[]{:S(2)}) async-start(bf16[4,32,2560]{2,1,0:T(8,128)(2,1)} %reduce_sum.53), calls=%async_computation.2 | async-start | bytes 1310720 | tf_op jit(solution)/shard_map/all_to_all | solution.py:24
  184.8 21.1 %all-to-all-start.5 = ((bf16[4,32,2560]{2,1,0:T(8,128)(2,1)}), bf16[4,32,2560]{2,1,0:T(8,128)(2,1)}, u32[]{:S(2)}, u32[]{:S(2)}) async-start(bf16[4,32,2560]{2,1,0:T(8,128)(2,1)} %reduce_sum.55), calls=%async_computation.5 | async-start | bytes 1310720 | tf_op jit(solution)/shard_map/all_to_all | solution.py:24
  189.0 3.8 %copy-start.2 = (bf16[16,32,2560]{2,1,0:T(8,128)(2,1)S(1)}, bf16[16,32,2560]{2,1,0:T(8,128)(2,1)}, u32[]{:S(2)}) copy-start(bf16[16,32,2560]{2,1,0:T(8,128)(2,1)} %all-gather.3.cloned.1.call-done) | copy-start | bytes 7864324
  192.8 1.8 copy-start.8
  192.8 1.8 copy-start.11
  195.8 17.1 %collective-permute-start = (bf16[1,128,2560]{2,1,0:T(8,128)(2,1)}, bf16[1,128,2560]{2,1,0:T(8,128)(2,1)S(1)}, u32[]{:S(2)}, u32[]{:S(2)}) collective-permute-start(bf16[1,128,2560]{2,1,0:T(8,128)(2,1)} %fusion.6), channel_id=1, source_target_pairs={{0,16},{1,17},{2,18},{3,19},{4,20},{5,21},{6,22},{7,23},{8,24},{9,... | collective-permute-start | bytes 1966088 | tf_op jit(solution)/shard_map/ppermute | solution.py:10
  207.3 17.6 %collective-permute-start.1 = (bf16[1,128,2560]{2,1,0:T(8,128)(2,1)S(1)}, bf16[1,128,2560]{2,1,0:T(8,128)(2,1)S(1)}, u32[]{:S(2)}, u32[]{:S(2)}) collective-permute-start(bf16[1,128,2560]{2,1,0:T(8,128)(2,1)S(1)} %fusion.7), channel_id=1, source_target_pairs={{16,0},{17,1},{18,2},{19,3},{20,4},{21,5},{22,6},{23,7},{24,8},{25... | collective-permute-start | bytes 1966088 | tf_op jit(solution)/shard_map/ppermute | solution.py:10
Sparse Core Ops, SparseCore 0:
  34.4 24.6 all-gather.2
  60.7 25.5 all-gather.4
where the time goes:
time: 234 us; the launch traced here: 233 us
  waiting for transfers between devices  115 us (49%)
  blocking collectives  43.2 us (18%)
  matrix products  26.4 us (11%)
  starting transfers between devices  22.7 us (10%)
  between operations  14.3 us (6%)
  other arithmetic  10 us (4%)
    all_to_all x2, waiting for transfers between devices, to_owners(): lax.all_to_all(partial_value, 'dp', split_axis=0, concat_axis=0, tiled=True)  54.8 us
    all_to_all x2, blocking collectives, to_experts(): lax.all_to_all(buffer, 'expert', split_axis=0, concat_axis=0, tiled=True)  43.2 us
    all_gather x2, waiting for transfers between devices, to_experts(): arrived = lax.all_gather(columns, 'dp', axis=0, tiled=True)  27.2 us
    all_to_all x2, waiting for transfers between devices, to_owners(): lax.all_to_all(column_rows, 'expert', split_axis=0, concat_axis=0, tiled=...  20.5 us
    ppermute x2, waiting for transfers between devices, passed_along(): lax.ppermute(value, axis, [(source, source + steps) for source in range(f...  12 us
    all_to_all x2, starting transfers between devices, to_owners(): lax.all_to_all(partial_value, 'dp', split_axis=0, concat_axis=0, tiled=True)  9.2 us
    all_to_all x2, starting transfers between devices, to_owners(): lax.all_to_all(column_rows, 'expert', split_axis=0, concat_axis=0, tiled=...  8.76 us
    reduce_sum x2, other arithmetic, to_owners(): column_rows = jnp.sum(quarters.astype(jnp.float32), 0).astype(jnp.bfloat16)  6.29 us
  transfers between devices with their start and end apart: 8, of which 7 were waited for; matrix products, arithmetic and copies ran while one was open for 12% of the time, Pallas kernels for 0%

commit v1 on v0

--- a/solution.py
+++ b/solution.py
@@ -12,7 +12,9 @@
 
 def to_experts(buffer):
     columns = lax.all_to_all(buffer, "expert", split_axis=0, concat_axis=0, tiled=True)
-    arrived = lax.all_gather(columns, "dp", axis=0, tiled=True)
+    arrived = jnp.concatenate(
+        lax.all_to_all(jnp.stack([columns] * lax.axis_size("dp")), "dp", 0, 0), axis=0
+    )
     return arrived
 
 

time: 234 us -> 262 us (1.12)
  waiting for transfers between devices: 115 us -> 131 us
  between operations: 14.3 us -> 0.89 us
  blocking collectives: 43.2 us -> 53.8 us
  starting transfers between devices: 22.7 us -> 32.4 us
    all_to_all x0 -> x2, waiting for transfers between devices: none -> 43.7 us  [the longest x1 26.8 us: to_experts(): lax.all_to_all(jnp.stack([columns] * lax.axis_size('dp')), 'dp', 0, 0)]
    all_to_all x0 -> x1, blocking collectives: none -> 34.6 us  [to_experts(): lax.all_to_all(jnp.stack([columns] * lax.axis_size('dp')), 'dp', 0, 0)]
    all_gather x2 -> x0, waiting for transfers between devices: 27.2 us -> none  [to_experts(): arrived = lax.all_gather(columns, 'dp', axis=0, tiled=True)]
    all_to_all x2 -> x1, blocking collectives: 43.2 us -> 19.3 us  [to_experts(): lax.all_to_all(buffer, 'expert', split_axis=0, concat_axis=0, tiled=True)]
    all_to_all x0 -> x2, starting transfers between devices: none -> 10.9 us  [the longest x1 6.35 us: to_experts(): lax.all_to_all(buffer, 'expert', split_axis=0, concat_axis=0, tiled=True)]
  transfers between devices with their start and end apart: 8 -> 8, of which waited for: 7 -> 7; matrix products, arithmetic and copies ran while one was open for 12% -> 11% of each run, Pallas kernels for 0% -> 0%
where the time goes in v1:
time: 262 us; the launch traced here: 261 us
  waiting for transfers between devices  131 us (50%)
  blocking collectives  53.8 us (21%)
  starting transfers between devices  32.4 us (12%)
  matrix products  27.2 us (10%)
  other arithmetic  10.8 us (4%)
  local copies, waits for them, and re-layouts  4.29 us (2%)
    all_to_all x2, waiting for transfers between devices, to_owners(): lax.all_to_all(partial_value, 'dp', split_axis=0, concat_axis=0, tiled=True)  54.8 us
    all_to_all x1, blocking collectives, to_experts(): lax.all_to_all(jnp.stack([columns] * lax.axis_size('dp')), 'dp', 0, 0)  34.6 us
    all_to_all x1, waiting for transfers between devices, to_experts(): lax.all_to_all(jnp.stack([columns] * lax.axis_size('dp')), 'dp', 0, 0)  26.8 us
    all_to_all x2, waiting for transfers between devices, to_owners(): lax.all_to_all(column_rows, 'expert', split_axis=0, concat_axis=0, tiled=...  20.7 us
    all_to_all x1, blocking collectives, to_experts(): lax.all_to_all(buffer, 'expert', split_axis=0, concat_axis=0, tiled=True)  19.3 us
    all_to_all x1, waiting for transfers between devices, to_experts(): lax.all_to_all(buffer, 'expert', split_axis=0, concat_axis=0, tiled=True)  17 us
    ppermute x2, waiting for transfers between devices, passed_along(): lax.ppermute(value, axis, [(source, source + steps) for source in range(f...  12 us
    all_to_all x2, starting transfers between devices, to_owners(): lax.all_to_all(partial_value, 'dp', split_axis=0, concat_axis=0, tiled=True)  9.18 us
  transfers between devices with their start and end apart: 8, of which 7 were waited for; matrix products, arithmetic and copies ran while one was open for 11% of the time, Pallas kernels for 0%

profile of v1, /device:TPU:0, one launch (start us, length us, event | category | flops | bytes accessed | tf_op | source)
XLA Modules:
  0.0 260.7 jit_solution(10953851252642300491)
XLA Ops:
  5.8 6.3 %all-to-all-start.4 = ((bf16[4,32,2560]{2,1,0:T(8,128)(2,1)}), bf16[4,32,2560]{2,1,0:T(8,128)(2,1)S(1)}, u32[]{:S(2)}, u32[]{:S(2)}) async-start(bf16[4,32,2560]{2,1,0:T(8,128)(2,1)} %bitcast.12), calls=%async_computation.4 | async-start | bytes 1310720 | tf_op jit(solution)/shard_map/all_to_all | solution.py:14
  12.4 17.0 %all-to-all-done.4 = bf16[4,32,2560]{2,1,0:T(8,128)(2,1)S(1)} async-done(((bf16[4,32,2560]{2,1,0:T(8,128)(2,1)}), bf16[4,32,2560]{2,1,0:T(8,128)(2,1)S(1)}, u32[]{:S(2)}, u32[]{:S(2)}) %all-to-all-start.4) | async-done | bytes 655392 | tf_op jit(solution)/shard_map/all_to_all | solution.py:14
  29.4 19.3 %all_to_all.40 = bf16[4,32,2560]{2,1,0:T(8,128)(2,1)S(1)} all-to-all(bf16[4,32,2560]{2,1,0:T(8,128)(2,1)S(1)} %bitcast.95), channel_id=1, replica_groups=mesh['section'=2,'dp'=4,'expert'=4] {'expert'}, dimensions={0} | all-to-all | bytes 1310720 | tf_op jit(solution)/shard_map/all_to_all | solution.py:14
  48.9 34.6 %all_to_all.41 = bf16[4,4,32,2560]{3,2,1,0:T(8,128)(2,1)} all-to-all(bf16[4,4,32,2560]{3,2,1,0:T(8,128)(2,1)S(1)} %stack.10), channel_id=1, replica_groups=mesh['section'=2,'dp'=4,'expert'=4] {'dp'}, dimensions={0} | all-to-all | bytes 5242880 | tf_op jit(solution)/shard_map/all_to_all | solution.py:16
  85.3 4.6 %all-to-all-start.5 = ((bf16[4,4,32,2560]{3,2,1,0:T(8,128)(2,1)}), bf16[4,4,32,2560]{3,2,1,0:T(8,128)(2,1)}, u32[]{:S(2)}, u32[]{:S(2)}) async-start(bf16[4,4,32,2560]{3,2,1,0:T(8,128)(2,1)} %stack.11), calls=%async_computation.5 | async-start | bytes 5242880 | tf_op jit(solution)/shard_map/all_to_all | solution.py:16
  89.8 3.1 %fusion.12 = f32[512,256]{1,0:T(8,128)S(1)} fusion(bf16[512,2560]{1,0:T(8,128)(2,1)} %bitcast.89, bf16[1,1,2,256,2560]{4,3,2,1,0:T(8,128)(2,1)} %param.10), kind=kOutput, calls=%fused_computation.22 | convolution fusion | flops 671088640 | bytes 4456448 | tf_op jit(solution)/shard_map/dot_general | solution.py:70
  94.4 26.8 %all-to-all-done.5 = bf16[4,4,32,2560]{3,2,1,0:T(8,128)(2,1)} async-done(((bf16[4,4,32,2560]{3,2,1,0:T(8,128)(2,1)}), bf16[4,4,32,2560]{3,2,1,0:T(8,128)(2,1)}, u32[]{:S(2)}, u32[]{:S(2)}) %all-to-all-start.5) | async-done | bytes 2621472 | tf_op jit(solution)/shard_map/all_to_all | solution.py:16
  121.2 2.7 %multiply_convert_fusion.1 = (bf16[512,256]{1,0:T(8,128)(2,1)S(1)}, bf16[512,256]{1,0:T(8,128)(2,1)S(1)}, bf16[512,256]{1,0:T(8,128)(2,1)S(1)}) fusion(f32[512,256]{1,0:T(8,128)S(1)} %fusion.16, f32[512,256]{1,0:T(8,128)S(1)} %fusion.12, bf16[512,2560]{1,0:T(8,128)(2,1)} %bitcast.13, bf16[1,1,256,2560]{3,2,1,0:T(8,128)(2,1)S(1)} %copy-done), kind=kOutput, calls=%fused_computation.36 | convolution fusion | flops 673054720 | bytes 5767168 | tf_op jit(solution)/shard_map/dot_general | solution.py:81
  123.9 2.3 convolution_convert_fusion
  126.2 4.6 %all-to-all-start.2 = ((bf16[16,32,2560]{2,1,0:T(8,128)(2,1)}), bf16[16,32,2560]{2,1,0:T(8,128)(2,1)}, u32[]{:S(2)}, u32[]{:S(2)}) async-start(bf16[16,32,2560]{2,1,0:T(8,128)(2,1)} %bitcast.93), calls=%async_computation.2 | async-start | bytes 5242880 | tf_op jit(solution)/shard_map/all_to_all | solution.py:23
  133.2 2.4 add_convert_fusion
  135.5 26.6 %all-to-all-done.2 = bf16[16,32,2560]{2,1,0:T(8,128)(2,1)} async-done(((bf16[16,32,2560]{2,1,0:T(8,128)(2,1)}), bf16[16,32,2560]{2,1,0:T(8,128)(2,1)}, u32[]{:S(2)}, u32[]{:S(2)}) %all-to-all-start.2) | async-done | bytes 2621472 | tf_op jit(solution)/shard_map/all_to_all | solution.py:23
  162.2 4.6 %all-to-all-start.6 = ((bf16[16,32,2560]{2,1,0:T(8,128)(2,1)}), bf16[16,32,2560]{2,1,0:T(8,128)(2,1)}, u32[]{:S(2)}, u32[]{:S(2)}) async-start(bf16[16,32,2560]{2,1,0:T(8,128)(2,1)} %bitcast.94), calls=%async_computation.6 | async-start | bytes 5242880 | tf_op jit(solution)/shard_map/all_to_all | solution.py:23
  166.8 3.1 %reduce_sum.53 = bf16[4,32,2560]{2,1,0:T(8,128)(2,1)} reduce(bf16[4,4,32,2560]{3,2,1,0:T(8,128)(2,1)} %bitcast.8, bf16[]{:T(256)} %constant.16.clone.1), dimensions={0}, to_apply=%region_4.5 | reduce | flops 983040 | bytes 3276802 | tf_op jit(solution)/shard_map/reduce_sum | solution.py:25
  169.9 28.2 %all-to-all-done.6 = bf16[16,32,2560]{2,1,0:T(8,128)(2,1)} async-done(((bf16[16,32,2560]{2,1,0:T(8,128)(2,1)}), bf16[16,32,2560]{2,1,0:T(8,128)(2,1)}, u32[]{:S(2)}, u32[]{:S(2)}) %all-to-all-start.6) | async-done | bytes 2621472 | tf_op jit(solution)/shard_map/all_to_all | solution.py:23
  198.1 3.5 %all-to-all-start.3 = ((bf16[4,32,2560]{2,1,0:T(8,128)(2,1)}), bf16[4,32,2560]{2,1,0:T(8,128)(2,1)S(1)}, u32[]{:S(2)}, u32[]{:S(2)}) async-start(bf16[4,32,2560]{2,1,0:T(8,128)(2,1)} %reduce_sum.53), calls=%async_computation.3 | async-start | bytes 1310720 | tf_op jit(solution)/shard_map/all_to_all | solution.py:26
  201.6 3.1 %reduce_sum.55 = bf16[4,32,2560]{2,1,0:T(8,128)(2,1)} reduce(bf16[4,4,32,2560]{3,2,1,0:T(8,128)(2,1)} %bitcast.15, bf16[]{:T(256)} %constant.16.clone.1), dimensions={0}, to_apply=%region_6.7 | reduce | flops 983040 | bytes 3276802 | tf_op jit(solution)/shard_map/reduce_sum | solution.py:25
  204.7 14.1 %all-to-all-done.3 = bf16[4,32,2560]{2,1,0:T(8,128)(2,1)S(1)} async-done(((bf16[4,32,2560]{2,1,0:T(8,128)(2,1)}), bf16[4,32,2560]{2,1,0:T(8,128)(2,1)S(1)}, u32[]{:S(2)}, u32[]{:S(2)}) %all-to-all-start.3) | async-done | bytes 655392 | tf_op jit(solution)/shard_map/all_to_all | solution.py:26
  218.8 4.2 %all-to-all-start.7 = ((bf16[4,32,2560]{2,1,0:T(8,128)(2,1)}), bf16[4,32,2560]{2,1,0:T(8,128)(2,1)}, u32[]{:S(2)}, u32[]{:S(2)}) async-start(bf16[4,32,2560]{2,1,0:T(8,128)(2,1)} %reduce_sum.55), calls=%async_computation.7 | async-start | bytes 1310720 | tf_op jit(solution)/shard_map/all_to_all | solution.py:26
  223.0 3.8 %fusion.2 = bf16[1,1,256,2560]{3,2,1,0:T(8,128)(2,1)} fusion(bf16[512,256]{1,0:T(8,128)(2,1)S(1)} %get-tuple-element.6, bf16[512,2560]{1,0:T(8,128)(2,1)} %bitcast.13), kind=kOutput, calls=%fused_computation.7 | convolution fusion | flops 671744000 | bytes 4194304 | tf_op jit(solution)/shard_map/dot_general | solution.py:84
  229.9 3.4 %collective-permute-start = (bf16[1,128,2560]{2,1,0:T(8,128)(2,1)}, bf16[1,128,2560]{2,1,0:T(8,128)(2,1)S(1)}, u32[]{:S(2)}, u32[]{:S(2)}) collective-permute-start(bf16[1,128,2560]{2,1,0:T(8,128)(2,1)} %fusion.6), channel_id=1, source_target_pairs={{0,16},{1,17},{2,18},{3,19},{4,20},{5,21},{6,22},{7,23},{8,24},{9,... | collective-permute-start | bytes 1966088 | tf_op jit(solution)/shard_map/ppermute | solution.py:10
  233.3 6.6 %all-to-all-done.7 = bf16[4,32,2560]{2,1,0:T(8,128)(2,1)} async-done(((bf16[4,32,2560]{2,1,0:T(8,128)(2,1)}), bf16[4,32,2560]{2,1,0:T(8,128)(2,1)}, u32[]{:S(2)}, u32[]{:S(2)}) %all-to-all-start.7) | async-done | bytes 655392 | tf_op jit(solution)/shard_map/all_to_all | solution.py:26
  242.7 2.6 fusion
  247.0 12.0 %collective-permute-done.1 = bf16[1,128,2560]{2,1,0:T(8,128)(2,1)S(1)} collective-permute-done((bf16[1,128,2560]{2,1,0:T(8,128)(2,1)S(1)}, bf16[1,128,2560]{2,1,0:T(8,128)(2,1)S(1)}, u32[]{:S(2)}, u32[]{:S(2)}) %collective-permute-start.1) | collective-permute-done | bytes 655392 | tf_op jit(solution)/shard_map/ppermute | solution.py:10
  (45 shorter events, 20.3 us)
Async XLA Ops:
  0.6 120.5 %copy-start = (bf16[1,1,256,2560]{3,2,1,0:T(8,128)(2,1)S(1)}, bf16[1,1,256,2560]{3,2,1,0:T(8,128)(2,1)}, u32[]{:S(2)}) copy-start(bf16[1,1,256,2560]{3,2,1,0:T(8,128)(2,1)} %param.11) | copy-start | bytes 3932164
  0.6 11.5 %copy-start.6 = (bf16[1,128,2560]{2,1,0:T(8,128)(2,1)S(1)}, bf16[1,128,2560]{2,1,0:T(8,128)(2,1)}, u32[]{:S(2)}) copy-start(bf16[1,128,2560]{2,1,0:T(8,128)(2,1)} %param.6) | copy-start | bytes 1966084
  2.2 46.5 %copy-start.7 = (f32[4,128]{1,0:T(4,128)}, f32[4,128]{1,0:T(4,128)S(1)}, u32[]{:S(2)}) copy-start(f32[4,128]{1,0:T(4,128)S(1)} %fusion.33) | copy-start | bytes 6148
  3.0 45.6 %copy-start.9 = (f32[128]{0:T(128)}, f32[128]{0:T(128)S(1)}, u32[]{:S(2)}) copy-start(f32[128]{0:T(128)S(1)} %fusion.30) | copy-start | bytes 1540
  5.8 23.6 %all-to-all-start.4 = ((bf16[4,32,2560]{2,1,0:T(8,128)(2,1)}), bf16[4,32,2560]{2,1,0:T(8,128)(2,1)S(1)}, u32[]{:S(2)}, u32[]{:S(2)}) async-start(bf16[4,32,2560]{2,1,0:T(8,128)(2,1)} %bitcast.12), calls=%async_computation.4 | async-start | bytes 1310720 | tf_op jit(solution)/shard_map/all_to_all | solution.py:14
  85.3 35.9 %all-to-all-start.5 = ((bf16[4,4,32,2560]{3,2,1,0:T(8,128)(2,1)}), bf16[4,4,32,2560]{3,2,1,0:T(8,128)(2,1)}, u32[]{:S(2)}, u32[]{:S(2)}) async-start(bf16[4,4,32,2560]{3,2,1,0:T(8,128)(2,1)} %stack.11), calls=%async_computation.5 | async-start | bytes 5242880 | tf_op jit(solution)/shard_map/all_to_all | solution.py:16
  89.8 3.2 %copy-start.1 = (bf16[4,4,32,2560]{3,2,1,0:T(8,128)(2,1)S(1)}, bf16[4,4,32,2560]{3,2,1,0:T(8,128)(2,1)}, u32[]{:S(2)}) copy-start(bf16[4,4,32,2560]{3,2,1,0:T(8,128)(2,1)} %all_to_all.41) | copy-start | bytes 7864324
  89.8 3.7 %copy-start.3 = (bf16[1,1,2,256,2560]{4,3,2,1,0:T(8,128)(2,1)S(1)}, bf16[1,1,2,256,2560]{4,3,2,1,0:T(8,128)(2,1)}, u32[]{:S(2)}) copy-start(bf16[1,1,2,256,2560]{4,3,2,1,0:T(8,128)(2,1)} %param.10) | copy-start | bytes 7864324
  123.9 9.3 %copy-start.5 = (bf16[512,256]{1,0:T(8,128)(2,1)}, bf16[512,256]{1,0:T(8,128)(2,1)S(1)}, u32[]{:S(2)}) copy-start(bf16[512,256]{1,0:T(8,128)(2,1)S(1)} %get-tuple-element.4) | copy-start | bytes 786436
  126.2 35.9 %all-to-all-start.2 = ((bf16[16,32,2560]{2,1,0:T(8,128)(2,1)}), bf16[16,32,2560]{2,1,0:T(8,128)(2,1)}, u32[]{:S(2)}, u32[]{:S(2)}) async-start(bf16[16,32,2560]{2,1,0:T(8,128)(2,1)} %bitcast.93), calls=%async_computation.2 | async-start | bytes 5242880 | tf_op jit(solution)/shard_map/all_to_all | solution.py:23
  130.8 2.3 copy-start.4
  162.2 35.9 %all-to-all-start.6 = ((bf16[16,32,2560]{2,1,0:T(8,128)(2,1)}), bf16[16,32,2560]{2,1,0:T(8,128)(2,1)}, u32[]{:S(2)}, u32[]{:S(2)}) async-start(bf16[16,32,2560]{2,1,0:T(8,128)(2,1)} %bitcast.94), calls=%async_computation.6 | async-start | bytes 5242880 | tf_op jit(solution)/shard_map/all_to_all | solution.py:23
  198.1 20.7 %all-to-all-start.3 = ((bf16[4,32,2560]{2,1,0:T(8,128)(2,1)}), bf16[4,32,2560]{2,1,0:T(8,128)(2,1)S(1)}, u32[]{:S(2)}, u32[]{:S(2)}) async-start(bf16[4,32,2560]{2,1,0:T(8,128)(2,1)} %reduce_sum.53), calls=%async_computation.3 | async-start | bytes 1310720 | tf_op jit(solution)/shard_map/all_to_all | solution.py:26
  218.8 21.1 %all-to-all-start.7 = ((bf16[4,32,2560]{2,1,0:T(8,128)(2,1)}), bf16[4,32,2560]{2,1,0:T(8,128)(2,1)}, u32[]{:S(2)}, u32[]{:S(2)}) async-start(bf16[4,32,2560]{2,1,0:T(8,128)(2,1)} %reduce_sum.55), calls=%async_computation.7 | async-start | bytes 1310720 | tf_op jit(solution)/shard_map/all_to_all | solution.py:26
  223.0 3.8 %copy-start.2 = (bf16[4,4,32,2560]{3,2,1,0:T(8,128)(2,1)S(1)}, bf16[4,4,32,2560]{3,2,1,0:T(8,128)(2,1)}, u32[]{:S(2)}) copy-start(bf16[4,4,32,2560]{3,2,1,0:T(8,128)(2,1)} %all_to_all.41) | copy-start | bytes 7864324
  226.8 1.8 copy-start.8
  226.8 1.8 copy-start.10
  229.9 17.1 %collective-permute-start = (bf16[1,128,2560]{2,1,0:T(8,128)(2,1)}, bf16[1,128,2560]{2,1,0:T(8,128)(2,1)S(1)}, u32[]{:S(2)}, u32[]{:S(2)}) collective-permute-start(bf16[1,128,2560]{2,1,0:T(8,128)(2,1)} %fusion.6), channel_id=1, source_target_pairs={{0,16},{1,17},{2,18},{3,19},{4,20},{5,21},{6,22},{7,23},{8,24},{9,... | collective-permute-start | bytes 1966088 | tf_op jit(solution)/shard_map/ppermute | solution.py:10
  241.4 17.6 %collective-permute-start.1 = (bf16[1,128,2560]{2,1,0:T(8,128)(2,1)S(1)}, bf16[1,128,2560]{2,1,0:T(8,128)(2,1)S(1)}, u32[]{:S(2)}, u32[]{:S(2)}) collective-permute-start(bf16[1,128,2560]{2,1,0:T(8,128)(2,1)S(1)} %fusion.7), channel_id=1, source_target_pairs={{16,0},{17,1},{18,2},{19,3},{20,4},{21,5},{22,6},{23,7},{24,8},{25... | collective-permute-start | bytes 1966088 | tf_op jit(solution)/shard_map/ppermute | solution.py:10
